TPU v7x, 128 devices: a whole 4x4x4 slice. The times are simulated.
128 devices in a mesh: row: 8 (over z, y_hi), col: 16 (over y_lo, x, core).
Axes of the slice: x: 4, y: 4 (y_hi: 2, y_lo: 2; y = y_hi * 2 + y_lo), z: 4, core: 2. Of those that a mesh axis runs over, the one named last changes fastest.
Arguments:
- ancestor: float32 [16384, 16384], P('row', 'col'), may hold values from -6 to 6
- factor: float32 [2, 16384, 512], P(None, ('row', 'col')), may hold values from -0.0625 to 0.0625
- diag_inverse: float32 [2, 512, 512], replicated, may hold values from -6 to 6
- structure: int32 [2, 16], replicated, may hold values from 0 to 31, as said below
Outputs:
- off_diagonal: float32 [2, 16384, 512], P(None, ('row', 'col'))
- diag_block: float32 [2, 512, 512], replicated
Inputs may be any that keep to these rules, and one draw needn't show every extreme that they name: `structure`: each row holds 16 distinct tile indices; tile t covers rows t * 512 to t * 512 + 511.
All inputs are finite; a program needn't handle non-finite values.
Results may differ from a plain program's by a relative error of at most 0.0001.
Values sent between devices are 32-bit elements; how exact they have to be, the bound alone decides.
No kernel may reach another device: no remote copies, remote signals or barrier semaphores. Data moves between devices by JAX's collectives and lax.ppermute only.
A program may use at most 128 MiB of HBM per device.

v0:
```python
import jax
import jax.numpy as jnp
from jax import lax
from jax.experimental import pallas as pl
from jax.experimental.pallas import tpu as pltpu
from jax.sharding import Mesh
from jax.sharding import PartitionSpec as P

TILE = 512
WIDTH = 512

ROW, COL = ("z", "yh"), ("yl", "x", "core")
AXES, CHIPS = ROW + COL, ROW + COL[:2]


def route(move):
    pairs = []
    for d in range(128):
        z, yh, yl, x, core = d // 32, d // 16 % 2, d // 8 % 2, d // 2 % 4, d % 2
        z, y, x, core = move(z, yh * 2 + yl, x, core)
        z, y, x = z % 4, y % 4, x % 4
        pairs.append((d, z * 32 + (y // 2) * 16 + (y % 2) * 8 + x * 2 + core))
    return pairs


def to_core(v):
    return lax.ppermute(v, AXES, route(lambda z, y, x, c: (z, y, x, 1 - c)))


def to_x(v, s):
    return lax.ppermute(v, AXES, route(lambda z, y, x, c: (z, y, x + s, c)))


def to_y(v, s):
    return lax.ppermute(v, AXES, route(lambda z, y, x, c: (z, y + s, x, c)))


def to_yl(v):
    return lax.ppermute(v, AXES, route(lambda z, y, x, c: (z, y ^ 1, x, c)))


def to_z(v, s):
    return lax.ppermute(v, AXES, route(lambda z, y, x, c: (z + s, y, x, c)))


def halves(a):
    hi = a.astype(jnp.bfloat16)
    return hi, (a - hi.astype(jnp.float32)).astype(jnp.bfloat16)


def panel_kernel(info, own, oth, f0, f1, f2, f3, g_own, g_oth, *rest):
    outs, (f_hi, f_lo, acc, tiles, sems) = rest[:6], rest[6:]
    core, z, yh, x, yl = info[8], info[9], info[10], info[11], info[12]

    def each(i, act):
        rows = pl.ds(pl.multiple_of(i * TILE, TILE), TILE)
        for s, (ref, side) in enumerate(((own, core), (oth, 1 - core))):
            for j in range(2):
                slot, tile = s * 2 + j, side * 2 + j
                copy = pltpu.make_async_copy(
                    ref.at[rows, pl.ds(j * TILE, TILE)], tiles.at[i, slot], sems.at[i, slot]
                )

                @pl.when((info[i] > 0) & (info[4 + tile] > 0))
                def _():
                    act(copy, slot, tile)

    @pl.loop(0, 4)
    def _(i):
        each(i, lambda copy, slot, tile: copy.start())

    def place(value, col, row):
        at = pl.ds(pl.multiple_of(col * 128 + row * 16, 16), 16)
        hi, lo = halves(value)
        f_hi[at, :] = hi
        f_lo[at, :] = lo

    for s, ref in enumerate((f0, f1, f2, f3)):
        from_z = lax.rem(z + 4 - s, 4)
        for h, from_yh in enumerate((yh, 1 - yh)):
            for col in range(8):
                place(ref[h, col], col, from_z * 2 + from_yh)

    for ref, from_yh in ((g_own, yh), (g_oth, 1 - yh)):
        for s in range(4):
            from_z = lax.rem(z + 4 - s, 4)
            for col in range(8):
                place(ref[s, col], col + 8, from_z * 2 + from_yh)

    @pl.loop(0, 4)
    def _(i):
        acc[...] = jnp.zeros_like(acc)

        def add(copy, slot, tile):
            copy.wait()
            at = pl.ds(pl.multiple_of(tile * TILE, TILE), TILE)
            hi, lo = halves(tiles[i, slot])
            b_hi = f_hi[at, :]
            acc[...] += (
                jnp.dot(hi, b_hi, preferred_element_type=jnp.float32)
                + jnp.dot(lo, b_hi, preferred_element_type=jnp.float32)
                + jnp.dot(hi, f_lo[at, :], preferred_element_type=jnp.float32)
            )

        each(i, add)
        to_l = lax.div(i, 2)
        for b in range(2):
            step = lax.rem(lax.rem(i, 2) * 2 + b + 4 - x, 4)
            first = acc[b * 256 : b * 256 + 128, :]
            last = acc[b * 256 + 128 : b * 256 + 256, :]
            for s in range(4):

                @pl.when(step == s)
                def _():
                    outs[s][to_l] = first

            @pl.when(to_l == yl)
            def _():
                outs[4][step] = last

            @pl.when(to_l != yl)
            def _():
                outs[5][step] = last


def in_vmem(n):
    return [pl.BlockSpec(memory_space=pltpu.VMEM)] * n


def panel(info, own, oth, pieces):
    cols = pieces[0].shape[-1]
    out = [jax.ShapeDtypeStruct((2, 128, cols), jnp.float32)] * 4
    out += [jax.ShapeDtypeStruct((4, 128, cols), jnp.float32)] * 2
    return pl.pallas_call(
        panel_kernel,
        in_specs=[pl.BlockSpec(memory_space=pltpu.SMEM)]
        + [pl.BlockSpec(memory_space=pl.ANY)] * 2
        + in_vmem(6),
        out_specs=in_vmem(6),
        scratch_shapes=[
            pltpu.VMEM((2048, cols), jnp.bfloat16),
            pltpu.VMEM((2048, cols), jnp.bfloat16),
            pltpu.VMEM((TILE, cols), jnp.float32),
            pltpu.VMEM((4, 4, TILE, TILE), jnp.float32),
            pltpu.SemaphoreType.DMA((4, 4)),
        ],
        out_shape=out,
        compiler_params=pltpu.CompilerParams(vmem_limit_bytes=48 << 20),
        cost_estimate=pl.CostEstimate(
            flops=3 * 2 * 2048 * 2048 * cols,
            bytes_accessed=20 << 20,
            transcendentals=0,
        ),
    )(info, own, oth, *pieces)


def finish_kernel(info, *refs):
    parts, rows, (diag, keep, send, *lasts) = refs[:12], refs[12:18], refs[18:]
    yl = info[12]
    t_hi, t_lo = halves(jnp.concatenate([ref[...] for ref in rows], axis=1))
    for c in range(2):
        firsts, (mine, got) = parts[c * 6 : c * 6 + 4], parts[c * 6 + 4 : c * 6 + 6]
        here, away = (sum(ref[i] for ref in firsts) for i in (yl, 1 - yl))
        sums = [here, away] + [mine[s] + got[s] for s in range(4)]
        for ref, value in zip((keep, send, *lasts), sums):
            ref[c] = value
        p_hi, p_lo = halves(jnp.concatenate(sums, axis=0))
        cols = p_hi.shape[1]
        diag[:, c * cols : (c + 1) * cols] = (
            jnp.dot(t_hi, p_hi, preferred_element_type=jnp.float32)
            + jnp.dot(t_lo, p_hi, preferred_element_type=jnp.float32)
            + jnp.dot(t_hi, p_lo, preferred_element_type=jnp.float32)
        )


def finish(info, parts, rows):
    cols = parts[0].shape[-1]
    out = [jax.ShapeDtypeStruct((WIDTH, 2 * cols), jnp.float32)]
    out += [jax.ShapeDtypeStruct((2, 128, cols), jnp.float32)] * 6
    return pl.pallas_call(
        finish_kernel,
        in_specs=[pl.BlockSpec(memory_space=pltpu.SMEM)] + in_vmem(18),
        out_specs=in_vmem(7),
        out_shape=out,
        compiler_params=pltpu.CompilerParams(vmem_limit_bytes=24 << 20),
        cost_estimate=pl.CostEstimate(
            flops=3 * 4 * 768 * WIDTH * cols, bytes_accessed=9 << 20, transcendentals=0
        ),
    )(info, *parts, *rows)


def pick(v, i):
    return lax.dynamic_index_in_dim(v, i, 0, keepdims=False)


def per_device(ancestor, factor, diag_inverse, structure):
    z, yh, yl, x, core = (lax.axis_index(axis) for axis in AXES)
    row, group = z * 2 + yh, yl * 4 + x
    at_first = core == 0
    half = WIDTH // 2

    listed = pick(structure, core)
    four = jnp.arange(4, dtype=jnp.int32)
    flag = lambda tiles: jnp.any(listed[None, :] == tiles[:, None], axis=1)
    info = jnp.concatenate(
        [
            flag(row * 4 + four).astype(jnp.int32),
            flag(group * 4 + four).astype(jnp.int32),
            jnp.stack([core, z, yh, x, yl]).astype(jnp.int32),
        ]
    )

    oth = to_core(ancestor)

    turned = jnp.swapaxes(factor, 1, 2)
    f_keep = pick(turned, core)
    f_got = to_core(pick(turned, 1 - core))
    f_first = jnp.where(at_first, f_keep, f_got)
    f_last = jnp.where(at_first, f_got, f_keep)
    f_rows = [f_first, to_yl(f_first), f_last, *(to_x(f_last, s) for s in (3, 2, 1))]

    spread = lax.all_to_all(factor.reshape(2, 8, 16, WIDTH), ROW, 1, 0)
    spread = lax.all_to_all(spread.reshape(16, 16, WIDTH), COL, 0, 0)
    spread, info = lax.optimization_barrier((spread, info))
    gathered = []
    for c in range(2):
        low, high = (v[:, :, c * half : (c + 1) * half] for v in (spread[:8], spread[8:]))
        low_y, *high_z = lax.optimization_barrier(
            (to_y(low, 2), high, *(to_z(high, s) for s in (1, 2, 3)))
        )
        pair, quad = jnp.stack([low, low_y]), jnp.stack(high_z)
        pairs = [pair] + [to_z(pair, s) for s in (1, 2, 3)]
        gathered.append([*pairs, quad, to_y(quad, 2)])

    parts = []
    for c in range(2):
        first0, first1, first2, first3, last_keep, last_send = panel(
            info, ancestor, oth, gathered[c]
        )
        got = [to_x(first1, 1), to_x(first3, 3), to_x(first2, 2)]
        parts += [first0, *got, last_keep, to_yl(last_send)]

    diag, first, first_send, *last = finish(info, parts, f_rows)
    first = first + to_yl(first_send)
    last = last[0] + to_x(last[1], 1) + to_x(last[3], 3) + to_x(last[2], 2)
    mine = jnp.where(at_first, first, last)
    theirs = to_core(jnp.where(at_first, last, first))
    off = -jnp.where(at_first, jnp.stack([mine, theirs]), jnp.stack([theirs, mine]))
    off = jnp.concatenate([off[:, 0], off[:, 1]], axis=-1)

    diag = lax.all_to_all(diag.reshape(64, 8, WIDTH), CHIPS, 0, 0)
    own8 = ((row * 2 + yl) * 4 + x) * 8
    diag = jnp.sum(diag, axis=0)
    diag = diag + lax.dynamic_slice(diag_inverse, (core, own8, 0), (1, 8, WIDTH))[0]
    diag = lax.all_to_all(jnp.broadcast_to(diag, (64, 8, WIDTH)), CHIPS, 0, 0)
    diag = diag.reshape(WIDTH, WIDTH)
    diag_oth = to_core(diag)
    both = jnp.where(
        at_first, jnp.stack([diag, diag_oth]), jnp.stack([diag_oth, diag])
    )
    return off, both


def solution(mesh):
    mesh = Mesh(mesh.devices.reshape(4, 2, 2, 4, 2), AXES)
    in_specs = (P(ROW, COL), P(None, AXES, None), P(), P())
    out_specs = (P(None, AXES, None), P())

    return jax.shard_map(
        per_device, mesh=mesh, in_specs=in_specs, out_specs=out_specs, check_vma=False
    )
```

profile of v0, /device:TPU:1, one launch (start us, length us, event | category | flops | bytes accessed | tf_op | source)
XLA Modules:
  0.0 190.1 jit_solution(11148118425388370352)
XLA Ops:
  3.3 19.1 %all_to_all.30 = f32[1,2,8,16,512]{4,3,1,0,2:T(8,128)} all-to-all(f32[1,2,8,16,512]{4,3,1,0,2:T(8,128)S(1)} %copy.17), channel_id=1, replica_groups=mesh['z'=4,'yh'=2,'yl'=2,'x'=4,'core'=2] {'z','yh'}, dimensions={2} | all-to-all | bytes 1048576 | tf_op jit(solution)/shard_map/all_to_all | solution.py:222
  22.3 5.6 %all-to-all-start.1 = ((f32[16,16,512]{2,1,0:T(8,128)}), f32[16,16,512]{2,1,0:T(8,128)S(1)}, u32[]{:S(2)}, u32[]{:S(2)}) async-start(f32[16,16,512]{2,1,0:T(8,128)} %bitcast.3), calls=%async_computation.1 | async-start | bytes 1048576 | tf_op jit(solution)/shard_map/all_to_all | solution.py:223
  28.3 9.1 %all-to-all-done.1 = f32[16,16,512]{2,1,0:T(8,128)S(1)} async-done(((f32[16,16,512]{2,1,0:T(8,128)}), f32[16,16,512]{2,1,0:T(8,128)S(1)}, u32[]{:S(2)}, u32[]{:S(2)}) %all-to-all-start.1) | async-done | bytes 524320 | tf_op jit(solution)/shard_map/all_to_all | solution.py:223
  37.8 1.7 collective-permute-start.25
  39.5 1.8 collective-permute-start.15
  43.8 2.6 %collective-permute-done.15 = f32[8,16,256]{2,1,0:T(8,128)S(1)} collective-permute-done((f32[8,16,256]{2,1,0:T(8,128)S(1)}, f32[8,16,256]{2,1,0:T(8,128)S(1)}, u32[]{:S(2)}, u32[]{:S(2)}) %collective-permute-start.15) | collective-permute-done | bytes 131104 | tf_op jit(solution)/shard_map/ppermute | solution.py:43
  46.6 2.5 %collective-permute-done.16 = f32[8,16,256]{2,1,0:T(8,128)S(1)} collective-permute-done((f32[8,16,256]{2,1,0:T(8,128)S(1)}, f32[8,16,256]{2,1,0:T(8,128)S(1)}, u32[]{:S(2)}, u32[]{:S(2)}) %collective-permute-start.16) | collective-permute-done | bytes 131104 | tf_op jit(solution)/shard_map/ppermute | solution.py:43
  50.1 2.1 %collective-permute-start.4 = (f32[8,16,256]{2,1,0:T(8,128)S(1)}, f32[8,16,256]{2,1,0:T(8,128)S(1)}, u32[]{:S(2)}, u32[]{:S(2)}) collective-permute-start(f32[8,16,256]{2,1,0:T(8,128)S(1)} %get-tuple-element.36), channel_id=1, source_target_pairs={{0,96},{1,97},{2,98},{3,99},{4,100},{5,101},{6,102},{7,103},{8,104... | collective-permute-start | bytes 393224 | tf_op jit(solution)/shard_map/ppermute | solution.py:43
  53.2 2.1 %collective-permute-start.20 = (f32[4,8,16,256]{3,2,1,0:T(8,128)S(1)}, f32[4,8,16,256]{3,2,1,0:T(8,128)S(1)}, u32[]{:S(2)}, u32[]{:S(2)}) collective-permute-start(f32[4,8,16,256]{3,2,1,0:T(8,128)S(1)} %pad_maximum_fusion.1.g_own), channel_id=1, source_target_pairs={{0,16},{1,17},{2,18},{3,19},{4,20},{5,21},{6,22},{7,23},{8,24},{9,... | collective-permute-start | bytes 1572872 | tf_op jit(solution)/shard_map/ppermute | solution.py:35
  56.2 1.8 collective-permute-done.4
  59.3 2.3 %collective-permute-start.19 = (f32[2,8,16,256]{3,2,1,0:T(8,128)S(1)}, f32[2,8,16,256]{3,2,1,0:T(8,128)S(1)}, u32[]{:S(2)}, u32[]{:S(2)}) collective-permute-start(f32[2,8,16,256]{3,2,1,0:T(8,128)S(1)} %pad_maximum_fusion.4.f0), channel_id=1, source_target_pairs={{0,96},{1,97},{2,98},{3,99},{4,100},{5,101},{6,102},{7,103},{8,104... | collective-permute-start | bytes 786440 | tf_op jit(solution)/shard_map/ppermute | solution.py:43
  61.7 1.9 collective-permute-done.17.f1
  63.6 10.2 %collective-permute-start.27 = (f32[512,128]{1,0:T(8,128)S(1)}, f32[512,128]{1,0:T(8,128)S(1)}, u32[]{:S(2)}, u32[]{:S(2)}) collective-permute-start(f32[512,128]{1,0:T(8,128)S(1)} %get-tuple-element.70.refs_14_), channel_id=1, source_target_pairs={{0,6},{1,7},{2,0},{3,1},{4,2},{5,3},{6,4},{7,5},{8,14},{9,15},{10,... | collective-permute-start | bytes 786440 | tf_op jit(solution)/shard_map/ppermute | solution.py:31
  74.2 2.8 %collective-permute-start.7 = (f32[2,8,16,256]{3,2,1,0:T(8,128)S(1)}, f32[2,8,16,256]{3,2,1,0:T(8,128)S(1)}, u32[]{:S(2)}, u32[]{:S(2)}) collective-permute-start(f32[2,8,16,256]{3,2,1,0:T(8,128)S(1)} %pad_maximum_fusion.3.f0), channel_id=1, source_target_pairs={{0,96},{1,97},{2,98},{3,99},{4,100},{5,101},{6,102},{7,103},{8,104... | collective-permute-start | bytes 786440 | tf_op jit(solution)/shard_map/ppermute | solution.py:43
  78.0 4.6 %shard_map.60 = (f32[2,128,256]{2,1,0:T(8,128)S(1)}, f32[2,128,256]{2,1,0:T(8,128)S(1)}, f32[2,128,256]{2,1,0:T(8,128)S(1)}, f32[2,128,256]{2,1,0:T(8,128)S(1)},...) custom-call(s32[13]{0:T(128)S(1)} %concatenate.6.info, f32[2048,1024]{1,0:T(8,128)} %own.3, ...), custom_call_target="tpu_custom_call" | custom-call | flops 6442450944 | bytes 20971520 | tf_op jit(solution)/shard_map/pallas_call | solution.py:134
  82.7 4.8 %collective-permute-done.5.f1 = f32[2,8,16,256]{3,2,1,0:T(8,128)S(1)} collective-permute-done((f32[2,8,16,256]{3,2,1,0:T(8,128)S(1)}, f32[2,8,16,256]{3,2,1,0:T(8,128)S(1)}, u32[]{:S(2)}, u32[]{:S(2)}) %collective-permute-start.5) | collective-permute-done | bytes 262176 | tf_op jit(solution)/shard_map/ppermute | solution.py:43
  90.8 4.6 %shard_map.59 = (f32[2,128,256]{2,1,0:T(8,128)S(1)}, f32[2,128,256]{2,1,0:T(8,128)S(1)}, f32[2,128,256]{2,1,0:T(8,128)S(1)}, f32[2,128,256]{2,1,0:T(8,128)S(1)},...) custom-call(s32[13]{0:T(128)S(1)} %concatenate.6.info, f32[2048,1024]{1,0:T(8,128)} %own.3, ...), custom_call_target="tpu_custom_call" | custom-call | flops 6442450944 | bytes 20971520 | tf_op jit(solution)/shard_map/pallas_call | solution.py:134
  95.8 1.5 collective-permute-start.23
  97.3 5.4 %collective-permute-done.29.refs_17_ = f32[512,128]{1,0:T(8,128)S(1)} collective-permute-done((f32[512,128]{1,0:T(8,128)S(1)}, f32[512,128]{1,0:T(8,128)S(1)}, u32[]{:S(2)}, u32[]{:S(2)}) %collective-permute-start.29) | collective-permute-done | bytes 262176 | tf_op jit(solution)/shard_map/ppermute | solution.py:31
  104.3 6.4 %collective-permute-done.21.refs_7_ = f32[2,128,256]{2,1,0:T(8,128)S(1)} collective-permute-done((f32[2,128,256]{2,1,0:T(8,128)S(1)}, f32[2,128,256]{2,1,0:T(8,128)S(1)}, u32[]{:S(2)}, u32[]{:S(2)}) %collective-permute-start.21) | collective-permute-done | bytes 262176 | tf_op jit(solution)/shard_map/ppermute | solution.py:31
  112.2 5.7 %collective-permute-done.10.refs_2_ = f32[2,128,256]{2,1,0:T(8,128)S(1)} collective-permute-done((f32[2,128,256]{2,1,0:T(8,128)S(1)}, f32[2,128,256]{2,1,0:T(8,128)S(1)}, u32[]{:S(2)}, u32[]{:S(2)}) %collective-permute-start.10) | collective-permute-done | bytes 262176 | tf_op jit(solution)/shard_map/ppermute | solution.py:31
  118.8 7.2 %collective-permute-done.9.refs_1_ = f32[2,128,256]{2,1,0:T(8,128)S(1)} collective-permute-done((f32[2,128,256]{2,1,0:T(8,128)S(1)}, f32[2,128,256]{2,1,0:T(8,128)S(1)}, u32[]{:S(2)}, u32[]{:S(2)}) %collective-permute-start.9) | collective-permute-done | bytes 262176 | tf_op jit(solution)/shard_map/ppermute | solution.py:31
  126.9 3.1 %shard_map.61 = (f32[512,512]{1,0:T(8,128)}, f32[2,128,256]{2,1,0:T(8,128)S(1)}, f32[2,128,256]{2,1,0:T(8,128)S(1)}, f32[2,128,256]{2,1,0:T(8,128)S(1)}, f32[2,1...) custom-call(s32[13]{0:T(128)S(1)} %concatenate.6.info, ...), custom_call_target="tpu_custom_call" | custom-call | flops 1207959552 | bytes 9437184 | tf_op jit(solution)/shard_map/pallas_call | solution.py:180
  130.0 4.7 %all-to-all-start.2 = ((f32[64,8,512]{2,1,0:T(8,128)}), f32[64,8,512]{2,1,0:T(8,128)S(1)}, u32[]{:S(2)}, u32[]{:S(2)}) async-start(f32[64,8,512]{2,1,0:T(8,128)} %bitcast.31), calls=%async_computation.2 | async-start | bytes 2097152 | tf_op jit(solution)/shard_map/all_to_all | solution.py:251
  134.7 17.2 %all-to-all-done.2 = f32[64,8,512]{2,1,0:T(8,128)S(1)} async-done(((f32[64,8,512]{2,1,0:T(8,128)}), f32[64,8,512]{2,1,0:T(8,128)S(1)}, u32[]{:S(2)}, u32[]{:S(2)}) %all-to-all-start.2) | async-done | bytes 1048608 | tf_op jit(solution)/shard_map/all_to_all | solution.py:251
  153.8 4.8 %all-to-all-start.3 = ((f32[64,8,512]{2,1,0:T(8,128)}), f32[64,8,512]{2,1,0:T(8,128)S(1)}, u32[]{:S(2)}, u32[]{:S(2)}) async-start(f32[64,8,512]{2,1,0:T(8,128)} %broadcast_in_dim.2), calls=%async_computation.3 | async-start | bytes 2097152 | tf_op jit(solution)/shard_map/all_to_all | solution.py:255
  160.9 1.5 collective-permute-start.32
  162.4 1.5 collective-permute-start.33
  163.9 10.9 %all-to-all-done.3 = f32[64,8,512]{2,1,0:T(8,128)S(1)} async-done(((f32[64,8,512]{2,1,0:T(8,128)}), f32[64,8,512]{2,1,0:T(8,128)S(1)}, u32[]{:S(2)}, u32[]{:S(2)}) %all-to-all-start.3) | async-done | bytes 1048608 | tf_op jit(solution)/shard_map/all_to_all | solution.py:255
  174.8 6.5 %collective-permute-start.35 = (f32[512,512]{1,0:T(8,128)S(1)}, f32[512,512]{1,0:T(8,128)S(1)}, u32[]{:S(2)}, u32[]{:S(2)}) collective-permute-start(f32[512,512]{1,0:T(8,128)S(1)} %bitcast.50), channel_id=1, source_target_pairs={{0,1},{1,0},{2,3},{3,2},{4,5},{5,4},{6,7},{7,6},{8,9},{9,8},{10,11... | collective-permute-start | bytes 3145736 | tf_op jit(solution)/shard_map/ppermute | solution.py:27
  182.7 3.7 %collective-permute-start.34 = (f32[2,128,256]{2,1,0:T(8,128)S(1)}, f32[2,128,256]{2,1,0:T(8,128)S(1)}, u32[]{:S(2)}, u32[]{:S(2)}) collective-permute-start(f32[2,128,256]{2,1,0:T(8,128)S(1)} %broadcast_select_fusion), channel_id=1, source_target_pairs={{0,1},{1,0},{2,3},{3,2},{4,5},{5,4},{6,7},{7,6},{8,9},{9,8},{10,11... | collective-permute-start | bytes 786440 | tf_op jit(solution)/shard_map/ppermute | solution.py:27
  188.5 1.6 maximum_select_fusion
  (79 shorter events, 28.0 us)
Async XLA Ops:
  0.6 76.3 %collective-permute-start = (f32[2048,1024]{1,0:T(8,128)}, f32[2048,1024]{1,0:T(8,128)}, u32[]{:S(2)}, u32[]{:S(2)}) collective-permute-start(f32[2048,1024]{1,0:T(8,128)} %own.3), channel_id=1, source_target_pairs={{0,1},{1,0},{2,3},{3,2},{4,5},{5,4},{6,7},{7,6},{8,9},{9,8},{10,11... | collective-permute-start | bytes 25165832 | tf_op jit(solution)/shard_map/ppermute | solution.py:27
  22.3 15.1 %all-to-all-start.1 = ((f32[16,16,512]{2,1,0:T(8,128)}), f32[16,16,512]{2,1,0:T(8,128)S(1)}, u32[]{:S(2)}, u32[]{:S(2)}) async-start(f32[16,16,512]{2,1,0:T(8,128)} %bitcast.3), calls=%async_computation.1 | async-start | bytes 1048576 | tf_op jit(solution)/shard_map/all_to_all | solution.py:223
  37.8 14.4 %collective-permute-start.25 = (f32[512,128]{1,0:T(8,128)S(1)}, f32[512,128]{1,0:T(8,128)S(1)}, u32[]{:S(2)}, u32[]{:S(2)}) collective-permute-start(f32[512,128]{1,0:T(8,128)S(1)} %bitcast.56), channel_id=1, source_target_pairs={{0,1},{1,0},{2,3},{3,2},{4,5},{5,4},{6,7},{7,6},{8,9},{9,8},{10,11... | collective-permute-start | bytes 786440 | tf_op jit(solution)/shard_map/ppermute | solution.py:27
  41.3 7.8 %collective-permute-start.16 = (f32[8,16,256]{2,1,0:T(8,128)S(1)}, f32[8,16,256]{2,1,0:T(8,128)S(1)}, u32[]{:S(2)}, u32[]{:S(2)}) collective-permute-start(f32[8,16,256]{2,1,0:T(8,128)S(1)} %get-tuple-element.47), channel_id=1, source_target_pairs={{0,96},{1,97},{2,98},{3,99},{4,100},{5,101},{6,102},{7,103},{8,104... | collective-permute-start | bytes 393224 | tf_op jit(solution)/shard_map/ppermute | solution.py:43
  42.6 7.5 %collective-permute-start.13 = (f32[8,16,256]{2,1,0:T(8,128)S(1)}, f32[8,16,256]{2,1,0:T(8,128)S(1)}, u32[]{:S(2)}, u32[]{:S(2)}) collective-permute-start(f32[8,16,256]{2,1,0:T(8,128)S(1)} %get-tuple-element.77), channel_id=1, source_target_pairs={{0,16},{1,17},{2,18},{3,19},{4,20},{5,21},{6,22},{7,23},{8,24},{9,... | collective-permute-start | bytes 393224 | tf_op jit(solution)/shard_map/ppermute | solution.py:35
  50.1 7.8 %collective-permute-start.4 = (f32[8,16,256]{2,1,0:T(8,128)S(1)}, f32[8,16,256]{2,1,0:T(8,128)S(1)}, u32[]{:S(2)}, u32[]{:S(2)}) collective-permute-start(f32[8,16,256]{2,1,0:T(8,128)S(1)} %get-tuple-element.36), channel_id=1, source_target_pairs={{0,96},{1,97},{2,98},{3,99},{4,100},{5,101},{6,102},{7,103},{8,104... | collective-permute-start | bytes 393224 | tf_op jit(solution)/shard_map/ppermute | solution.py:43
  53.2 21.0 %collective-permute-start.20 = (f32[4,8,16,256]{3,2,1,0:T(8,128)S(1)}, f32[4,8,16,256]{3,2,1,0:T(8,128)S(1)}, u32[]{:S(2)}, u32[]{:S(2)}) collective-permute-start(f32[4,8,16,256]{3,2,1,0:T(8,128)S(1)} %pad_maximum_fusion.1.g_own), channel_id=1, source_target_pairs={{0,16},{1,17},{2,18},{3,19},{4,20},{5,21},{6,22},{7,23},{8,24},{9,... | collective-permute-start | bytes 1572872 | tf_op jit(solution)/shard_map/ppermute | solution.py:35
  56.2 7.4 %collective-permute-start.17 = (f32[2,8,16,256]{3,2,1,0:T(8,128)S(1)}, f32[2,8,16,256]{3,2,1,0:T(8,128)S(1)}, u32[]{:S(2)}, u32[]{:S(2)}) collective-permute-start(f32[2,8,16,256]{3,2,1,0:T(8,128)S(1)} %pad_maximum_fusion.4.f0), channel_id=1, source_target_pairs={{0,32},{1,33},{2,34},{3,35},{4,36},{5,37},{6,38},{7,39},{8,40},{9,... | collective-permute-start | bytes 786440 | tf_op jit(solution)/shard_map/ppermute | solution.py:43
  58.0 15.9 %collective-permute-start.18 = (f32[2,8,16,256]{3,2,1,0:T(8,128)S(1)}, f32[2,8,16,256]{3,2,1,0:T(8,128)S(1)}, u32[]{:S(2)}, u32[]{:S(2)}) collective-permute-start(f32[2,8,16,256]{3,2,1,0:T(8,128)S(1)} %pad_maximum_fusion.4.f0), channel_id=1, source_target_pairs={{0,64},{1,65},{2,66},{3,67},{4,68},{5,69},{6,70},{7,71},{8,72},{9,... | collective-permute-start | bytes 786440 | tf_op jit(solution)/shard_map/ppermute | solution.py:43
  59.3 14.6 %collective-permute-start.19 = (f32[2,8,16,256]{3,2,1,0:T(8,128)S(1)}, f32[2,8,16,256]{3,2,1,0:T(8,128)S(1)}, u32[]{:S(2)}, u32[]{:S(2)}) collective-permute-start(f32[2,8,16,256]{3,2,1,0:T(8,128)S(1)} %pad_maximum_fusion.4.f0), channel_id=1, source_target_pairs={{0,96},{1,97},{2,98},{3,99},{4,100},{5,101},{6,102},{7,103},{8,104... | collective-permute-start | bytes 786440 | tf_op jit(solution)/shard_map/ppermute | solution.py:43
  63.6 31.8 %collective-permute-start.27 = (f32[512,128]{1,0:T(8,128)S(1)}, f32[512,128]{1,0:T(8,128)S(1)}, u32[]{:S(2)}, u32[]{:S(2)}) collective-permute-start(f32[512,128]{1,0:T(8,128)S(1)} %get-tuple-element.70.refs_14_), channel_id=1, source_target_pairs={{0,6},{1,7},{2,0},{3,1},{4,2},{5,3},{6,4},{7,5},{8,14},{9,15},{10,... | collective-permute-start | bytes 786440 | tf_op jit(solution)/shard_map/ppermute | solution.py:31
  73.8 13.6 %collective-permute-start.5 = (f32[2,8,16,256]{3,2,1,0:T(8,128)S(1)}, f32[2,8,16,256]{3,2,1,0:T(8,128)S(1)}, u32[]{:S(2)}, u32[]{:S(2)}) collective-permute-start(f32[2,8,16,256]{3,2,1,0:T(8,128)S(1)} %pad_maximum_fusion.3.f0), channel_id=1, source_target_pairs={{0,32},{1,33},{2,34},{3,35},{4,36},{5,37},{6,38},{7,39},{8,40},{9,... | collective-permute-start | bytes 786440 | tf_op jit(solution)/shard_map/ppermute | solution.py:43
  73.9 14.0 %collective-permute-start.6 = (f32[2,8,16,256]{3,2,1,0:T(8,128)S(1)}, f32[2,8,16,256]{3,2,1,0:T(8,128)S(1)}, u32[]{:S(2)}, u32[]{:S(2)}) collective-permute-start(f32[2,8,16,256]{3,2,1,0:T(8,128)S(1)} %pad_maximum_fusion.3.f0), channel_id=1, source_target_pairs={{0,64},{1,65},{2,66},{3,67},{4,68},{5,69},{6,70},{7,71},{8,72},{9,... | collective-permute-start | bytes 786440 | tf_op jit(solution)/shard_map/ppermute | solution.py:43
  74.2 14.3 %collective-permute-start.7 = (f32[2,8,16,256]{3,2,1,0:T(8,128)S(1)}, f32[2,8,16,256]{3,2,1,0:T(8,128)S(1)}, u32[]{:S(2)}, u32[]{:S(2)}) collective-permute-start(f32[2,8,16,256]{3,2,1,0:T(8,128)S(1)} %pad_maximum_fusion.3.f0), channel_id=1, source_target_pairs={{0,96},{1,97},{2,98},{3,99},{4,100},{5,101},{6,102},{7,103},{8,104... | collective-permute-start | bytes 786440 | tf_op jit(solution)/shard_map/ppermute | solution.py:43
  77.0 12.6 %collective-permute-start.8 = (f32[4,8,16,256]{3,2,1,0:T(8,128)S(1)}, f32[4,8,16,256]{3,2,1,0:T(8,128)S(1)}, u32[]{:S(2)}, u32[]{:S(2)}) collective-permute-start(f32[4,8,16,256]{3,2,1,0:T(8,128)S(1)} %pad_maximum_fusion.g_own), channel_id=1, source_target_pairs={{0,16},{1,17},{2,18},{3,19},{4,20},{5,21},{6,22},{7,23},{8,24},{9,... | collective-permute-start | bytes 1572872 | tf_op jit(solution)/shard_map/ppermute | solution.py:35
  87.4 8.4 %collective-permute-start.28 = (f32[512,128]{1,0:T(8,128)S(1)}, f32[512,128]{1,0:T(8,128)S(1)}, u32[]{:S(2)}, u32[]{:S(2)}) collective-permute-start(f32[512,128]{1,0:T(8,128)S(1)} %get-tuple-element.70.refs_14_), channel_id=1, source_target_pairs={{0,4},{1,5},{2,6},{3,7},{4,0},{5,1},{6,2},{7,3},{8,12},{9,13},{10,... | collective-permute-start | bytes 786440 | tf_op jit(solution)/shard_map/ppermute | solution.py:31
  87.8 15.0 %collective-permute-start.29 = (f32[512,128]{1,0:T(8,128)S(1)}, f32[512,128]{1,0:T(8,128)S(1)}, u32[]{:S(2)}, u32[]{:S(2)}) collective-permute-start(f32[512,128]{1,0:T(8,128)S(1)} %get-tuple-element.70.refs_14_), channel_id=1, source_target_pairs={{0,2},{1,3},{2,4},{3,5},{4,6},{5,7},{6,0},{7,1},{8,10},{9,11},{10,... | collective-permute-start | bytes 786440 | tf_op jit(solution)/shard_map/ppermute | solution.py:31
  88.5 14.3 %collective-permute-start.26 = (f32[512,128]{1,0:T(8,128)S(1)}, f32[512,128]{1,0:T(8,128)S(1)}, u32[]{:S(2)}, u32[]{:S(2)}) collective-permute-start(f32[512,128]{1,0:T(8,128)S(1)} %get-tuple-element.71.refs_12_), channel_id=1, source_target_pairs={{0,8},{1,9},{2,10},{3,11},{4,12},{5,13},{6,14},{7,15},{8,0},{9,1},... | collective-permute-start | bytes 786440 | tf_op jit(solution)/shard_map/ppermute | solution.py:39
  89.6 21.1 %collective-permute-start.21 = (f32[2,128,256]{2,1,0:T(8,128)S(1)}, f32[2,128,256]{2,1,0:T(8,128)S(1)}, u32[]{:S(2)}, u32[]{:S(2)}) collective-permute-start(f32[2,128,256]{2,1,0:T(8,128)S(1)} %get-tuple-element.52), channel_id=1, source_target_pairs={{0,2},{1,3},{2,4},{3,5},{4,6},{5,7},{6,0},{7,1},{8,10},{9,11},{10,... | collective-permute-start | bytes 786440 | tf_op jit(solution)/shard_map/ppermute | solution.py:31
  95.5 15.2 %collective-permute-start.22 = (f32[2,128,256]{2,1,0:T(8,128)S(1)}, f32[2,128,256]{2,1,0:T(8,128)S(1)}, u32[]{:S(2)}, u32[]{:S(2)}) collective-permute-start(f32[2,128,256]{2,1,0:T(8,128)S(1)} %get-tuple-element.53), channel_id=1, source_target_pairs={{0,6},{1,7},{2,0},{3,1},{4,2},{5,3},{6,4},{7,5},{8,14},{9,15},{10,... | collective-permute-start | bytes 786440 | tf_op jit(solution)/shard_map/ppermute | solution.py:31
  95.8 16.0 %collective-permute-start.23 = (f32[2,128,256]{2,1,0:T(8,128)S(1)}, f32[2,128,256]{2,1,0:T(8,128)S(1)}, u32[]{:S(2)}, u32[]{:S(2)}) collective-permute-start(f32[2,128,256]{2,1,0:T(8,128)S(1)} %get-tuple-element.54), channel_id=1, source_target_pairs={{0,4},{1,5},{2,6},{3,7},{4,0},{5,1},{6,2},{7,3},{8,12},{9,13},{10,... | collective-permute-start | bytes 786440 | tf_op jit(solution)/shard_map/ppermute | solution.py:31
  102.8 23.2 %collective-permute-start.24 = (f32[4,128,256]{2,1,0:T(8,128)S(1)}, f32[4,128,256]{2,1,0:T(8,128)S(1)}, u32[]{:S(2)}, u32[]{:S(2)}) collective-permute-start(f32[4,128,256]{2,1,0:T(8,128)S(1)} %get-tuple-element.56), channel_id=1, source_target_pairs={{0,8},{1,9},{2,10},{3,11},{4,12},{5,13},{6,14},{7,15},{8,0},{9,1},... | collective-permute-start | bytes 1572872 | tf_op jit(solution)/shard_map/ppermute | solution.py:39
  102.8 24.1 %collective-permute-start.12 = (f32[4,128,256]{2,1,0:T(8,128)S(1)}, f32[4,128,256]{2,1,0:T(8,128)S(1)}, u32[]{:S(2)}, u32[]{:S(2)}) collective-permute-start(f32[4,128,256]{2,1,0:T(8,128)S(1)} %get-tuple-element.45), channel_id=1, source_target_pairs={{0,8},{1,9},{2,10},{3,11},{4,12},{5,13},{6,14},{7,15},{8,0},{9,1},... | collective-permute-start | bytes 1572872 | tf_op jit(solution)/shard_map/ppermute | solution.py:39
  110.6 8.2 %collective-permute-start.11 = (f32[2,128,256]{2,1,0:T(8,128)S(1)}, f32[2,128,256]{2,1,0:T(8,128)S(1)}, u32[]{:S(2)}, u32[]{:S(2)}) collective-permute-start(f32[2,128,256]{2,1,0:T(8,128)S(1)} %get-tuple-element.43), channel_id=1, source_target_pairs={{0,4},{1,5},{2,6},{3,7},{4,0},{5,1},{6,2},{7,3},{8,12},{9,13},{10,... | collective-permute-start | bytes 786440 | tf_op jit(solution)/shard_map/ppermute | solution.py:31
  111.8 14.2 %collective-permute-start.9 = (f32[2,128,256]{2,1,0:T(8,128)S(1)}, f32[2,128,256]{2,1,0:T(8,128)S(1)}, u32[]{:S(2)}, u32[]{:S(2)}) collective-permute-start(f32[2,128,256]{2,1,0:T(8,128)S(1)} %get-tuple-element.41), channel_id=1, source_target_pairs={{0,2},{1,3},{2,4},{3,5},{4,6},{5,7},{6,0},{7,1},{8,10},{9,11},{10,... | collective-permute-start | bytes 786440 | tf_op jit(solution)/shard_map/ppermute | solution.py:31
  130.0 21.8 %all-to-all-start.2 = ((f32[64,8,512]{2,1,0:T(8,128)}), f32[64,8,512]{2,1,0:T(8,128)S(1)}, u32[]{:S(2)}, u32[]{:S(2)}) async-start(f32[64,8,512]{2,1,0:T(8,128)} %bitcast.31), calls=%async_computation.2 | async-start | bytes 2097152 | tf_op jit(solution)/shard_map/all_to_all | solution.py:251
  153.8 21.0 %all-to-all-start.3 = ((f32[64,8,512]{2,1,0:T(8,128)}), f32[64,8,512]{2,1,0:T(8,128)S(1)}, u32[]{:S(2)}, u32[]{:S(2)}) async-start(f32[64,8,512]{2,1,0:T(8,128)} %broadcast_in_dim.2), calls=%async_computation.3 | async-start | bytes 2097152 | tf_op jit(solution)/shard_map/all_to_all | solution.py:255
  158.6 22.6 %collective-permute-start.30 = (f32[2,128,256]{2,1,0:T(8,128)S(1)}, f32[2,128,256]{2,1,0:T(8,128)S(1)}, u32[]{:S(2)}, u32[]{:S(2)}) collective-permute-start(f32[2,128,256]{2,1,0:T(8,128)S(1)} %get-tuple-element.58), channel_id=1, source_target_pairs={{0,8},{1,9},{2,10},{3,11},{4,12},{5,13},{6,14},{7,15},{8,0},{9,1},... | collective-permute-start | bytes 786440 | tf_op jit(solution)/shard_map/ppermute | solution.py:39
  159.7 21.5 %collective-permute-start.31 = (f32[2,128,256]{2,1,0:T(8,128)S(1)}, f32[2,128,256]{2,1,0:T(8,128)S(1)}, u32[]{:S(2)}, u32[]{:S(2)}) collective-permute-start(f32[2,128,256]{2,1,0:T(8,128)S(1)} %get-tuple-element.60), channel_id=1, source_target_pairs={{0,2},{1,3},{2,4},{3,5},{4,6},{5,7},{6,0},{7,1},{8,10},{9,11},{10,... | collective-permute-start | bytes 786440 | tf_op jit(solution)/shard_map/ppermute | solution.py:31
  160.9 20.3 %collective-permute-start.32 = (f32[2,128,256]{2,1,0:T(8,128)S(1)}, f32[2,128,256]{2,1,0:T(8,128)S(1)}, u32[]{:S(2)}, u32[]{:S(2)}) collective-permute-start(f32[2,128,256]{2,1,0:T(8,128)S(1)} %get-tuple-element.61), channel_id=1, source_target_pairs={{0,6},{1,7},{2,0},{3,1},{4,2},{5,3},{6,4},{7,5},{8,14},{9,15},{10,... | collective-permute-start | bytes 786440 | tf_op jit(solution)/shard_map/ppermute | solution.py:31
  162.4 19.2 %collective-permute-start.33 = (f32[2,128,256]{2,1,0:T(8,128)S(1)}, f32[2,128,256]{2,1,0:T(8,128)}, u32[]{:S(2)}, u32[]{:S(2)}) collective-permute-start(f32[2,128,256]{2,1,0:T(8,128)S(1)} %get-tuple-element.62), channel_id=1, source_target_pairs={{0,4},{1,5},{2,6},{3,7},{4,0},{5,1},{6,2},{7,3},{8,12},{9,13},{10,... | collective-permute-start | bytes 786440 | tf_op jit(solution)/shard_map/ppermute | solution.py:31
  174.8 13.7 %collective-permute-start.35 = (f32[512,512]{1,0:T(8,128)S(1)}, f32[512,512]{1,0:T(8,128)S(1)}, u32[]{:S(2)}, u32[]{:S(2)}) collective-permute-start(f32[512,512]{1,0:T(8,128)S(1)} %bitcast.50), channel_id=1, source_target_pairs={{0,1},{1,0},{2,3},{3,2},{4,5},{5,4},{6,7},{7,6},{8,9},{9,8},{10,11... | collective-permute-start | bytes 3145736 | tf_op jit(solution)/shard_map/ppermute | solution.py:27
  (9 other events, 107.8 us)
where the time goes:
time: 191 us; the launch traced here: 190 us
  waiting for transfers between devices  82.2 us (43%)
  starting transfers between devices  68.1 us (36%)
  blocking collectives  19.1 us (10%)
  Pallas kernels  12.4 us (6%)
  other arithmetic  4.74 us (2%)
  local copies, waits for them, and re-layouts  2.77 us (1%)
    ppermute x12, waiting for transfers between devices, to_x(): return lax.ppermute(v, AXES, route(lambda z, y, x, c: (z, y, x + s, c)))  27.1 us
    all_to_all x1, blocking collectives, per_device(): spread = lax.all_to_all(factor.reshape(2, 8, 16, WIDTH), ROW, 1, 0)  19.1 us
    ppermute x12, starting transfers between devices, to_x(): return lax.ppermute(v, AXES, route(lambda z, y, x, c: (z, y, x + s, c)))  18.2 us
    all_to_all x1, waiting for transfers between devices, per_device(): diag = lax.all_to_all(diag.reshape(64, 8, WIDTH), CHIPS, 0, 0)  17.2 us
    ppermute x12, waiting for transfers between devices, to_z(): return lax.ppermute(v, AXES, route(lambda z, y, x, c: (z + s, y, x, c)))  15.1 us
    ppermute x4, starting transfers between devices, to_core(): return lax.ppermute(v, AXES, route(lambda z, y, x, c: (z, y, x, 1 - c)))  13.3 us
    ppermute x12, starting transfers between devices, to_z(): return lax.ppermute(v, AXES, route(lambda z, y, x, c: (z + s, y, x, c)))  13.1 us
    all_to_all x1, waiting for transfers between devices, per_device(): diag = lax.all_to_all(jnp.broadcast_to(diag, (64, 8, WIDTH)), CHIPS, 0, 0)  10.9 us
  transfers between devices with their start and end apart: 39, of which 21 were waited for; matrix products, arithmetic and copies ran while one was open for 2% of the time, Pallas kernels for 5%

commit v1 on v0

--- a/solution.py
+++ b/solution.py
@@ -75,17 +75,19 @@
         f_hi[at, :] = hi
         f_lo[at, :] = lo
 
-    for s, ref in enumerate((f0, f1, f2, f3)):
-        from_z = lax.rem(z + 4 - s, 4)
-        for h, from_yh in enumerate((yh, 1 - yh)):
-            for col in range(8):
-                place(ref[h, col], col, from_z * 2 + from_yh)
-
-    for ref, from_yh in ((g_own, yh), (g_oth, 1 - yh)):
-        for s in range(4):
-            from_z = lax.rem(z + 4 - s, 4)
-            for col in range(8):
-                place(ref[s, col], col + 8, from_z * 2 + from_yh)
+    for tile in range(4):
+
+        @pl.when(info[4 + tile] > 0)
+        def _():
+            for col in range(tile * 4, tile * 4 + 4):
+                for s in range(4):
+                    from_z = lax.rem(z + 4 - s, 4)
+                    for h, from_yh in enumerate((yh, 1 - yh)):
+                        if col < 8:
+                            piece = (f0, f1, f2, f3)[s][h, col]
+                        else:
+                            piece = (g_own, g_oth)[h][s, col - 8]
+                        place(piece, col, from_z * 2 + from_yh)
 
     @pl.loop(0, 4)
     def _(i):
@@ -145,7 +147,7 @@
             pltpu.SemaphoreType.DMA((4, 4)),
         ],
         out_shape=out,
-        compiler_params=pltpu.CompilerParams(vmem_limit_bytes=48 << 20),
+        compiler_params=pltpu.CompilerParams(vmem_limit_bytes=44 << 20),
         cost_estimate=pl.CostEstimate(
             flops=3 * 2 * 2048 * 2048 * cols,
             bytes_accessed=20 << 20,

time: 191 us -> 191 us (level)
  no operation moved by 1% of the time
where the time goes in v1:
time: 191 us; the launch traced here: 190 us
  waiting for transfers between devices  82.2 us (43%)
  starting transfers between devices  68.1 us (36%)
  blocking collectives  19.1 us (10%)
  Pallas kernels  12.4 us (6%)
  other arithmetic  4.74 us (2%)
  local copies, waits for them, and re-layouts  2.77 us (1%)
    ppermute x12, waiting for transfers between devices, to_x(): return lax.ppermute(v, AXES, route(lambda z, y, x, c: (z, y, x + s, c)))  27.1 us
    all_to_all x1, blocking collectives, per_device(): spread = lax.all_to_all(factor.reshape(2, 8, 16, WIDTH), ROW, 1, 0)  19.1 us
    ppermute x12, starting transfers between devices, to_x(): return lax.ppermute(v, AXES, route(lambda z, y, x, c: (z, y, x + s, c)))  18.2 us
    all_to_all x1, waiting for transfers between devices, per_device(): diag = lax.all_to_all(diag.reshape(64, 8, WIDTH), CHIPS, 0, 0)  17.2 us
    ppermute x12, waiting for transfers between devices, to_z(): return lax.ppermute(v, AXES, route(lambda z, y, x, c: (z + s, y, x, c)))  15.1 us
    ppermute x4, starting transfers between devices, to_core(): return lax.ppermute(v, AXES, route(lambda z, y, x, c: (z, y, x, 1 - c)))  13.3 us
    ppermute x12, starting transfers between devices, to_z(): return lax.ppermute(v, AXES, route(lambda z, y, x, c: (z + s, y, x, c)))  13.1 us
    all_to_all x1, waiting for transfers between devices, per_device(): diag = lax.all_to_all(jnp.broadcast_to(diag, (64, 8, WIDTH)), CHIPS, 0, 0)  10.9 us
  transfers between devices with their start and end apart: 39, of which 21 were waited for; matrix products, arithmetic and copies ran while one was open for 2% of the time, Pallas kernels for 5%

profile of v1, /device:TPU:1, one launch (start us, length us, event | category | flops | bytes accessed | tf_op | source)
XLA Modules:
  0.0 190.1 jit_solution(8005463598198246360)
XLA Ops:
  3.3 19.1 %all_to_all.30 = f32[1,2,8,16,512]{4,3,1,0,2:T(8,128)} all-to-all(f32[1,2,8,16,512]{4,3,1,0,2:T(8,128)S(1)} %copy.17), channel_id=1, replica_groups=mesh['z'=4,'yh'=2,'yl'=2,'x'=4,'core'=2] {'z','yh'}, dimensions={2} | all-to-all | bytes 1048576 | tf_op jit(solution)/shard_map/all_to_all | solution.py:224
  22.3 5.6 %all-to-all-start.1 = ((f32[16,16,512]{2,1,0:T(8,128)}), f32[16,16,512]{2,1,0:T(8,128)S(1)}, u32[]{:S(2)}, u32[]{:S(2)}) async-start(f32[16,16,512]{2,1,0:T(8,128)} %bitcast.3), calls=%async_computation.1 | async-start | bytes 1048576 | tf_op jit(solution)/shard_map/all_to_all | solution.py:225
  28.3 9.1 %all-to-all-done.1 = f32[16,16,512]{2,1,0:T(8,128)S(1)} async-done(((f32[16,16,512]{2,1,0:T(8,128)}), f32[16,16,512]{2,1,0:T(8,128)S(1)}, u32[]{:S(2)}, u32[]{:S(2)}) %all-to-all-start.1) | async-done | bytes 524320 | tf_op jit(solution)/shard_map/all_to_all | solution.py:225
  37.8 1.7 collective-permute-start.25
  39.5 1.8 collective-permute-start.15
  43.8 2.6 %collective-permute-done.15 = f32[8,16,256]{2,1,0:T(8,128)S(1)} collective-permute-done((f32[8,16,256]{2,1,0:T(8,128)S(1)}, f32[8,16,256]{2,1,0:T(8,128)S(1)}, u32[]{:S(2)}, u32[]{:S(2)}) %collective-permute-start.15) | collective-permute-done | bytes 131104 | tf_op jit(solution)/shard_map/ppermute | solution.py:43
  46.6 2.5 %collective-permute-done.16 = f32[8,16,256]{2,1,0:T(8,128)S(1)} collective-permute-done((f32[8,16,256]{2,1,0:T(8,128)S(1)}, f32[8,16,256]{2,1,0:T(8,128)S(1)}, u32[]{:S(2)}, u32[]{:S(2)}) %collective-permute-start.16) | collective-permute-done | bytes 131104 | tf_op jit(solution)/shard_map/ppermute | solution.py:43
  50.1 2.1 %collective-permute-start.4 = (f32[8,16,256]{2,1,0:T(8,128)S(1)}, f32[8,16,256]{2,1,0:T(8,128)S(1)}, u32[]{:S(2)}, u32[]{:S(2)}) collective-permute-start(f32[8,16,256]{2,1,0:T(8,128)S(1)} %get-tuple-element.36), channel_id=1, source_target_pairs={{0,96},{1,97},{2,98},{3,99},{4,100},{5,101},{6,102},{7,103},{8,104... | collective-permute-start | bytes 393224 | tf_op jit(solution)/shard_map/ppermute | solution.py:43
  53.2 2.1 %collective-permute-start.20 = (f32[4,8,16,256]{3,2,1,0:T(8,128)S(1)}, f32[4,8,16,256]{3,2,1,0:T(8,128)S(1)}, u32[]{:S(2)}, u32[]{:S(2)}) collective-permute-start(f32[4,8,16,256]{3,2,1,0:T(8,128)S(1)} %pad_maximum_fusion.1.g_own), channel_id=1, source_target_pairs={{0,16},{1,17},{2,18},{3,19},{4,20},{5,21},{6,22},{7,23},{8,24},{9,... | collective-permute-start | bytes 1572872 | tf_op jit(solution)/shard_map/ppermute | solution.py:35
  56.2 1.8 collective-permute-done.4
  59.3 2.3 %collective-permute-start.19 = (f32[2,8,16,256]{3,2,1,0:T(8,128)S(1)}, f32[2,8,16,256]{3,2,1,0:T(8,128)S(1)}, u32[]{:S(2)}, u32[]{:S(2)}) collective-permute-start(f32[2,8,16,256]{3,2,1,0:T(8,128)S(1)} %pad_maximum_fusion.4.f0), channel_id=1, source_target_pairs={{0,96},{1,97},{2,98},{3,99},{4,100},{5,101},{6,102},{7,103},{8,104... | collective-permute-start | bytes 786440 | tf_op jit(solution)/shard_map/ppermute | solution.py:43
  61.7 1.9 collective-permute-done.17.f1
  63.6 10.2 %collective-permute-start.27 = (f32[512,128]{1,0:T(8,128)S(1)}, f32[512,128]{1,0:T(8,128)S(1)}, u32[]{:S(2)}, u32[]{:S(2)}) collective-permute-start(f32[512,128]{1,0:T(8,128)S(1)} %get-tuple-element.70.refs_14_), channel_id=1, source_target_pairs={{0,6},{1,7},{2,0},{3,1},{4,2},{5,3},{6,4},{7,5},{8,14},{9,15},{10,... | collective-permute-start | bytes 786440 | tf_op jit(solution)/shard_map/ppermute | solution.py:31
  74.2 2.8 %collective-permute-start.7 = (f32[2,8,16,256]{3,2,1,0:T(8,128)S(1)}, f32[2,8,16,256]{3,2,1,0:T(8,128)S(1)}, u32[]{:S(2)}, u32[]{:S(2)}) collective-permute-start(f32[2,8,16,256]{3,2,1,0:T(8,128)S(1)} %pad_maximum_fusion.3.f0), channel_id=1, source_target_pairs={{0,96},{1,97},{2,98},{3,99},{4,100},{5,101},{6,102},{7,103},{8,104... | collective-permute-start | bytes 786440 | tf_op jit(solution)/shard_map/ppermute | solution.py:43
  78.0 4.6 %shard_map.60 = (f32[2,128,256]{2,1,0:T(8,128)S(1)}, f32[2,128,256]{2,1,0:T(8,128)S(1)}, f32[2,128,256]{2,1,0:T(8,128)S(1)}, f32[2,128,256]{2,1,0:T(8,128)S(1)},...) custom-call(s32[13]{0:T(128)S(1)} %concatenate.6.info, f32[2048,1024]{1,0:T(8,128)} %own.3, ...), custom_call_target="tpu_custom_call" | custom-call | flops 6442450944 | bytes 20971520 | tf_op jit(solution)/shard_map/pallas_call | solution.py:136
  82.7 4.8 %collective-permute-done.5.f1 = f32[2,8,16,256]{3,2,1,0:T(8,128)S(1)} collective-permute-done((f32[2,8,16,256]{3,2,1,0:T(8,128)S(1)}, f32[2,8,16,256]{3,2,1,0:T(8,128)S(1)}, u32[]{:S(2)}, u32[]{:S(2)}) %collective-permute-start.5) | collective-permute-done | bytes 262176 | tf_op jit(solution)/shard_map/ppermute | solution.py:43
  90.8 4.7 %shard_map.59 = (f32[2,128,256]{2,1,0:T(8,128)S(1)}, f32[2,128,256]{2,1,0:T(8,128)S(1)}, f32[2,128,256]{2,1,0:T(8,128)S(1)}, f32[2,128,256]{2,1,0:T(8,128)S(1)},...) custom-call(s32[13]{0:T(128)S(1)} %concatenate.6.info, f32[2048,1024]{1,0:T(8,128)} %own.3, ...), custom_call_target="tpu_custom_call" | custom-call | flops 6442450944 | bytes 20971520 | tf_op jit(solution)/shard_map/pallas_call | solution.py:136
  95.8 1.5 collective-permute-start.23
  97.3 5.4 %collective-permute-done.29.refs_17_ = f32[512,128]{1,0:T(8,128)S(1)} collective-permute-done((f32[512,128]{1,0:T(8,128)S(1)}, f32[512,128]{1,0:T(8,128)S(1)}, u32[]{:S(2)}, u32[]{:S(2)}) %collective-permute-start.29) | collective-permute-done | bytes 262176 | tf_op jit(solution)/shard_map/ppermute | solution.py:31
  104.3 6.4 %collective-permute-done.21.refs_7_ = f32[2,128,256]{2,1,0:T(8,128)S(1)} collective-permute-done((f32[2,128,256]{2,1,0:T(8,128)S(1)}, f32[2,128,256]{2,1,0:T(8,128)S(1)}, u32[]{:S(2)}, u32[]{:S(2)}) %collective-permute-start.21) | collective-permute-done | bytes 262176 | tf_op jit(solution)/shard_map/ppermute | solution.py:31
  112.2 5.7 %collective-permute-done.10.refs_2_ = f32[2,128,256]{2,1,0:T(8,128)S(1)} collective-permute-done((f32[2,128,256]{2,1,0:T(8,128)S(1)}, f32[2,128,256]{2,1,0:T(8,128)S(1)}, u32[]{:S(2)}, u32[]{:S(2)}) %collective-permute-start.10) | collective-permute-done | bytes 262176 | tf_op jit(solution)/shard_map/ppermute | solution.py:31
  118.8 7.2 %collective-permute-done.9.refs_1_ = f32[2,128,256]{2,1,0:T(8,128)S(1)} collective-permute-done((f32[2,128,256]{2,1,0:T(8,128)S(1)}, f32[2,128,256]{2,1,0:T(8,128)S(1)}, u32[]{:S(2)}, u32[]{:S(2)}) %collective-permute-start.9) | collective-permute-done | bytes 262176 | tf_op jit(solution)/shard_map/ppermute | solution.py:31
  126.9 3.1 %shard_map.61 = (f32[512,512]{1,0:T(8,128)}, f32[2,128,256]{2,1,0:T(8,128)S(1)}, f32[2,128,256]{2,1,0:T(8,128)S(1)}, f32[2,128,256]{2,1,0:T(8,128)S(1)}, f32[2,1...) custom-call(s32[13]{0:T(128)S(1)} %concatenate.6.info, ...), custom_call_target="tpu_custom_call" | custom-call | flops 1207959552 | bytes 9437184 | tf_op jit(solution)/shard_map/pallas_call | solution.py:182
  130.0 4.7 %all-to-all-start.2 = ((f32[64,8,512]{2,1,0:T(8,128)}), f32[64,8,512]{2,1,0:T(8,128)S(1)}, u32[]{:S(2)}, u32[]{:S(2)}) async-start(f32[64,8,512]{2,1,0:T(8,128)} %bitcast.31), calls=%async_computation.2 | async-start | bytes 2097152 | tf_op jit(solution)/shard_map/all_to_all | solution.py:253
  134.7 17.2 %all-to-all-done.2 = f32[64,8,512]{2,1,0:T(8,128)S(1)} async-done(((f32[64,8,512]{2,1,0:T(8,128)}), f32[64,8,512]{2,1,0:T(8,128)S(1)}, u32[]{:S(2)}, u32[]{:S(2)}) %all-to-all-start.2) | async-done | bytes 1048608 | tf_op jit(solution)/shard_map/all_to_all | solution.py:253
  153.8 4.8 %all-to-all-start.3 = ((f32[64,8,512]{2,1,0:T(8,128)}), f32[64,8,512]{2,1,0:T(8,128)S(1)}, u32[]{:S(2)}, u32[]{:S(2)}) async-start(f32[64,8,512]{2,1,0:T(8,128)} %broadcast_in_dim.2), calls=%async_computation.3 | async-start | bytes 2097152 | tf_op jit(solution)/shard_map/all_to_all | solution.py:257
  160.9 1.5 collective-permute-start.32
  162.4 1.5 collective-permute-start.33
  163.9 10.9 %all-to-all-done.3 = f32[64,8,512]{2,1,0:T(8,128)S(1)} async-done(((f32[64,8,512]{2,1,0:T(8,128)}), f32[64,8,512]{2,1,0:T(8,128)S(1)}, u32[]{:S(2)}, u32[]{:S(2)}) %all-to-all-start.3) | async-done | bytes 1048608 | tf_op jit(solution)/shard_map/all_to_all | solution.py:257
  174.8 6.5 %collective-permute-start.35 = (f32[512,512]{1,0:T(8,128)S(1)}, f32[512,512]{1,0:T(8,128)S(1)}, u32[]{:S(2)}, u32[]{:S(2)}) collective-permute-start(f32[512,512]{1,0:T(8,128)S(1)} %bitcast.50), channel_id=1, source_target_pairs={{0,1},{1,0},{2,3},{3,2},{4,5},{5,4},{6,7},{7,6},{8,9},{9,8},{10,11... | collective-permute-start | bytes 3145736 | tf_op jit(solution)/shard_map/ppermute | solution.py:27
  182.7 3.7 %collective-permute-start.34 = (f32[2,128,256]{2,1,0:T(8,128)S(1)}, f32[2,128,256]{2,1,0:T(8,128)S(1)}, u32[]{:S(2)}, u32[]{:S(2)}) collective-permute-start(f32[2,128,256]{2,1,0:T(8,128)S(1)} %broadcast_select_fusion), channel_id=1, source_target_pairs={{0,1},{1,0},{2,3},{3,2},{4,5},{5,4},{6,7},{7,6},{8,9},{9,8},{10,11... | collective-permute-start | bytes 786440 | tf_op jit(solution)/shard_map/ppermute | solution.py:27
  188.5 1.6 maximum_select_fusion
  (79 shorter events, 28.0 us)
Async XLA Ops:
  0.6 76.3 %collective-permute-start = (f32[2048,1024]{1,0:T(8,128)}, f32[2048,1024]{1,0:T(8,128)}, u32[]{:S(2)}, u32[]{:S(2)}) collective-permute-start(f32[2048,1024]{1,0:T(8,128)} %own.3), channel_id=1, source_target_pairs={{0,1},{1,0},{2,3},{3,2},{4,5},{5,4},{6,7},{7,6},{8,9},{9,8},{10,11... | collective-permute-start | bytes 25165832 | tf_op jit(solution)/shard_map/ppermute | solution.py:27
  22.3 15.1 %all-to-all-start.1 = ((f32[16,16,512]{2,1,0:T(8,128)}), f32[16,16,512]{2,1,0:T(8,128)S(1)}, u32[]{:S(2)}, u32[]{:S(2)}) async-start(f32[16,16,512]{2,1,0:T(8,128)} %bitcast.3), calls=%async_computation.1 | async-start | bytes 1048576 | tf_op jit(solution)/shard_map/all_to_all | solution.py:225
  37.8 14.4 %collective-permute-start.25 = (f32[512,128]{1,0:T(8,128)S(1)}, f32[512,128]{1,0:T(8,128)S(1)}, u32[]{:S(2)}, u32[]{:S(2)}) collective-permute-start(f32[512,128]{1,0:T(8,128)S(1)} %bitcast.56), channel_id=1, source_target_pairs={{0,1},{1,0},{2,3},{3,2},{4,5},{5,4},{6,7},{7,6},{8,9},{9,8},{10,11... | collective-permute-start | bytes 786440 | tf_op jit(solution)/shard_map/ppermute | solution.py:27
  41.3 7.8 %collective-permute-start.16 = (f32[8,16,256]{2,1,0:T(8,128)S(1)}, f32[8,16,256]{2,1,0:T(8,128)S(1)}, u32[]{:S(2)}, u32[]{:S(2)}) collective-permute-start(f32[8,16,256]{2,1,0:T(8,128)S(1)} %get-tuple-element.47), channel_id=1, source_target_pairs={{0,96},{1,97},{2,98},{3,99},{4,100},{5,101},{6,102},{7,103},{8,104... | collective-permute-start | bytes 393224 | tf_op jit(solution)/shard_map/ppermute | solution.py:43
  42.6 7.5 %collective-permute-start.13 = (f32[8,16,256]{2,1,0:T(8,128)S(1)}, f32[8,16,256]{2,1,0:T(8,128)S(1)}, u32[]{:S(2)}, u32[]{:S(2)}) collective-permute-start(f32[8,16,256]{2,1,0:T(8,128)S(1)} %get-tuple-element.77), channel_id=1, source_target_pairs={{0,16},{1,17},{2,18},{3,19},{4,20},{5,21},{6,22},{7,23},{8,24},{9,... | collective-permute-start | bytes 393224 | tf_op jit(solution)/shard_map/ppermute | solution.py:35
  50.1 7.8 %collective-permute-start.4 = (f32[8,16,256]{2,1,0:T(8,128)S(1)}, f32[8,16,256]{2,1,0:T(8,128)S(1)}, u32[]{:S(2)}, u32[]{:S(2)}) collective-permute-start(f32[8,16,256]{2,1,0:T(8,128)S(1)} %get-tuple-element.36), channel_id=1, source_target_pairs={{0,96},{1,97},{2,98},{3,99},{4,100},{5,101},{6,102},{7,103},{8,104... | collective-permute-start | bytes 393224 | tf_op jit(solution)/shard_map/ppermute | solution.py:43
  53.2 21.0 %collective-permute-start.20 = (f32[4,8,16,256]{3,2,1,0:T(8,128)S(1)}, f32[4,8,16,256]{3,2,1,0:T(8,128)S(1)}, u32[]{:S(2)}, u32[]{:S(2)}) collective-permute-start(f32[4,8,16,256]{3,2,1,0:T(8,128)S(1)} %pad_maximum_fusion.1.g_own), channel_id=1, source_target_pairs={{0,16},{1,17},{2,18},{3,19},{4,20},{5,21},{6,22},{7,23},{8,24},{9,... | collective-permute-start | bytes 1572872 | tf_op jit(solution)/shard_map/ppermute | solution.py:35
  56.2 7.4 %collective-permute-start.17 = (f32[2,8,16,256]{3,2,1,0:T(8,128)S(1)}, f32[2,8,16,256]{3,2,1,0:T(8,128)S(1)}, u32[]{:S(2)}, u32[]{:S(2)}) collective-permute-start(f32[2,8,16,256]{3,2,1,0:T(8,128)S(1)} %pad_maximum_fusion.4.f0), channel_id=1, source_target_pairs={{0,32},{1,33},{2,34},{3,35},{4,36},{5,37},{6,38},{7,39},{8,40},{9,... | collective-permute-start | bytes 786440 | tf_op jit(solution)/shard_map/ppermute | solution.py:43
  58.0 15.9 %collective-permute-start.18 = (f32[2,8,16,256]{3,2,1,0:T(8,128)S(1)}, f32[2,8,16,256]{3,2,1,0:T(8,128)S(1)}, u32[]{:S(2)}, u32[]{:S(2)}) collective-permute-start(f32[2,8,16,256]{3,2,1,0:T(8,128)S(1)} %pad_maximum_fusion.4.f0), channel_id=1, source_target_pairs={{0,64},{1,65},{2,66},{3,67},{4,68},{5,69},{6,70},{7,71},{8,72},{9,... | collective-permute-start | bytes 786440 | tf_op jit(solution)/shard_map/ppermute | solution.py:43
  59.3 14.6 %collective-permute-start.19 = (f32[2,8,16,256]{3,2,1,0:T(8,128)S(1)}, f32[2,8,16,256]{3,2,1,0:T(8,128)S(1)}, u32[]{:S(2)}, u32[]{:S(2)}) collective-permute-start(f32[2,8,16,256]{3,2,1,0:T(8,128)S(1)} %pad_maximum_fusion.4.f0), channel_id=1, source_target_pairs={{0,96},{1,97},{2,98},{3,99},{4,100},{5,101},{6,102},{7,103},{8,104... | collective-permute-start | bytes 786440 | tf_op jit(solution)/shard_map/ppermute | solution.py:43
  63.6 31.9 %collective-permute-start.27 = (f32[512,128]{1,0:T(8,128)S(1)}, f32[512,128]{1,0:T(8,128)S(1)}, u32[]{:S(2)}, u32[]{:S(2)}) collective-permute-start(f32[512,128]{1,0:T(8,128)S(1)} %get-tuple-element.70.refs_14_), channel_id=1, source_target_pairs={{0,6},{1,7},{2,0},{3,1},{4,2},{5,3},{6,4},{7,5},{8,14},{9,15},{10,... | collective-permute-start | bytes 786440 | tf_op jit(solution)/shard_map/ppermute | solution.py:31
  73.8 13.6 %collective-permute-start.5 = (f32[2,8,16,256]{3,2,1,0:T(8,128)S(1)}, f32[2,8,16,256]{3,2,1,0:T(8,128)S(1)}, u32[]{:S(2)}, u32[]{:S(2)}) collective-permute-start(f32[2,8,16,256]{3,2,1,0:T(8,128)S(1)} %pad_maximum_fusion.3.f0), channel_id=1, source_target_pairs={{0,32},{1,33},{2,34},{3,35},{4,36},{5,37},{6,38},{7,39},{8,40},{9,... | collective-permute-start | bytes 786440 | tf_op jit(solution)/shard_map/ppermute | solution.py:43
  73.9 14.0 %collective-permute-start.6 = (f32[2,8,16,256]{3,2,1,0:T(8,128)S(1)}, f32[2,8,16,256]{3,2,1,0:T(8,128)S(1)}, u32[]{:S(2)}, u32[]{:S(2)}) collective-permute-start(f32[2,8,16,256]{3,2,1,0:T(8,128)S(1)} %pad_maximum_fusion.3.f0), channel_id=1, source_target_pairs={{0,64},{1,65},{2,66},{3,67},{4,68},{5,69},{6,70},{7,71},{8,72},{9,... | collective-permute-start | bytes 786440 | tf_op jit(solution)/shard_map/ppermute | solution.py:43
  74.2 14.3 %collective-permute-start.7 = (f32[2,8,16,256]{3,2,1,0:T(8,128)S(1)}, f32[2,8,16,256]{3,2,1,0:T(8,128)S(1)}, u32[]{:S(2)}, u32[]{:S(2)}) collective-permute-start(f32[2,8,16,256]{3,2,1,0:T(8,128)S(1)} %pad_maximum_fusion.3.f0), channel_id=1, source_target_pairs={{0,96},{1,97},{2,98},{3,99},{4,100},{5,101},{6,102},{7,103},{8,104... | collective-permute-start | bytes 786440 | tf_op jit(solution)/shard_map/ppermute | solution.py:43
  77.0 12.6 %collective-permute-start.8 = (f32[4,8,16,256]{3,2,1,0:T(8,128)S(1)}, f32[4,8,16,256]{3,2,1,0:T(8,128)S(1)}, u32[]{:S(2)}, u32[]{:S(2)}) collective-permute-start(f32[4,8,16,256]{3,2,1,0:T(8,128)S(1)} %pad_maximum_fusion.g_own), channel_id=1, source_target_pairs={{0,16},{1,17},{2,18},{3,19},{4,20},{5,21},{6,22},{7,23},{8,24},{9,... | collective-permute-start | bytes 1572872 | tf_op jit(solution)/shard_map/ppermute | solution.py:35
  87.4 8.4 %collective-permute-start.28 = (f32[512,128]{1,0:T(8,128)S(1)}, f32[512,128]{1,0:T(8,128)S(1)}, u32[]{:S(2)}, u32[]{:S(2)}) collective-permute-start(f32[512,128]{1,0:T(8,128)S(1)} %get-tuple-element.70.refs_14_), channel_id=1, source_target_pairs={{0,4},{1,5},{2,6},{3,7},{4,0},{5,1},{6,2},{7,3},{8,12},{9,13},{10,... | collective-permute-start | bytes 786440 | tf_op jit(solution)/shard_map/ppermute | solution.py:31
  87.8 15.0 %collective-permute-start.29 = (f32[512,128]{1,0:T(8,128)S(1)}, f32[512,128]{1,0:T(8,128)S(1)}, u32[]{:S(2)}, u32[]{:S(2)}) collective-permute-start(f32[512,128]{1,0:T(8,128)S(1)} %get-tuple-element.70.refs_14_), channel_id=1, source_target_pairs={{0,2},{1,3},{2,4},{3,5},{4,6},{5,7},{6,0},{7,1},{8,10},{9,11},{10,... | collective-permute-start | bytes 786440 | tf_op jit(solution)/shard_map/ppermute | solution.py:31
  88.5 14.3 %collective-permute-start.26 = (f32[512,128]{1,0:T(8,128)S(1)}, f32[512,128]{1,0:T(8,128)S(1)}, u32[]{:S(2)}, u32[]{:S(2)}) collective-permute-start(f32[512,128]{1,0:T(8,128)S(1)} %get-tuple-element.71.refs_12_), channel_id=1, source_target_pairs={{0,8},{1,9},{2,10},{3,11},{4,12},{5,13},{6,14},{7,15},{8,0},{9,1},... | collective-permute-start | bytes 786440 | tf_op jit(solution)/shard_map/ppermute | solution.py:39
  89.6 21.1 %collective-permute-start.21 = (f32[2,128,256]{2,1,0:T(8,128)S(1)}, f32[2,128,256]{2,1,0:T(8,128)S(1)}, u32[]{:S(2)}, u32[]{:S(2)}) collective-permute-start(f32[2,128,256]{2,1,0:T(8,128)S(1)} %get-tuple-element.52), channel_id=1, source_target_pairs={{0,2},{1,3},{2,4},{3,5},{4,6},{5,7},{6,0},{7,1},{8,10},{9,11},{10,... | collective-permute-start | bytes 786440 | tf_op jit(solution)/shard_map/ppermute | solution.py:31
  95.5 15.2 %collective-permute-start.22 = (f32[2,128,256]{2,1,0:T(8,128)S(1)}, f32[2,128,256]{2,1,0:T(8,128)S(1)}, u32[]{:S(2)}, u32[]{:S(2)}) collective-permute-start(f32[2,128,256]{2,1,0:T(8,128)S(1)} %get-tuple-element.53), channel_id=1, source_target_pairs={{0,6},{1,7},{2,0},{3,1},{4,2},{5,3},{6,4},{7,5},{8,14},{9,15},{10,... | collective-permute-start | bytes 786440 | tf_op jit(solution)/shard_map/ppermute | solution.py:31
  95.8 16.0 %collective-permute-start.23 = (f32[2,128,256]{2,1,0:T(8,128)S(1)}, f32[2,128,256]{2,1,0:T(8,128)S(1)}, u32[]{:S(2)}, u32[]{:S(2)}) collective-permute-start(f32[2,128,256]{2,1,0:T(8,128)S(1)} %get-tuple-element.54), channel_id=1, source_target_pairs={{0,4},{1,5},{2,6},{3,7},{4,0},{5,1},{6,2},{7,3},{8,12},{9,13},{10,... | collective-permute-start | bytes 786440 | tf_op jit(solution)/shard_map/ppermute | solution.py:31
  102.8 23.2 %collective-permute-start.24 = (f32[4,128,256]{2,1,0:T(8,128)S(1)}, f32[4,128,256]{2,1,0:T(8,128)S(1)}, u32[]{:S(2)}, u32[]{:S(2)}) collective-permute-start(f32[4,128,256]{2,1,0:T(8,128)S(1)} %get-tuple-element.56), channel_id=1, source_target_pairs={{0,8},{1,9},{2,10},{3,11},{4,12},{5,13},{6,14},{7,15},{8,0},{9,1},... | collective-permute-start | bytes 1572872 | tf_op jit(solution)/shard_map/ppermute | solution.py:39
  102.8 24.1 %collective-permute-start.12 = (f32[4,128,256]{2,1,0:T(8,128)S(1)}, f32[4,128,256]{2,1,0:T(8,128)S(1)}, u32[]{:S(2)}, u32[]{:S(2)}) collective-permute-start(f32[4,128,256]{2,1,0:T(8,128)S(1)} %get-tuple-element.45), channel_id=1, source_target_pairs={{0,8},{1,9},{2,10},{3,11},{4,12},{5,13},{6,14},{7,15},{8,0},{9,1},... | collective-permute-start | bytes 1572872 | tf_op jit(solution)/shard_map/ppermute | solution.py:39
  110.6 8.2 %collective-permute-start.11 = (f32[2,128,256]{2,1,0:T(8,128)S(1)}, f32[2,128,256]{2,1,0:T(8,128)S(1)}, u32[]{:S(2)}, u32[]{:S(2)}) collective-permute-start(f32[2,128,256]{2,1,0:T(8,128)S(1)} %get-tuple-element.43), channel_id=1, source_target_pairs={{0,4},{1,5},{2,6},{3,7},{4,0},{5,1},{6,2},{7,3},{8,12},{9,13},{10,... | collective-permute-start | bytes 786440 | tf_op jit(solution)/shard_map/ppermute | solution.py:31
  111.8 14.2 %collective-permute-start.9 = (f32[2,128,256]{2,1,0:T(8,128)S(1)}, f32[2,128,256]{2,1,0:T(8,128)S(1)}, u32[]{:S(2)}, u32[]{:S(2)}) collective-permute-start(f32[2,128,256]{2,1,0:T(8,128)S(1)} %get-tuple-element.41), channel_id=1, source_target_pairs={{0,2},{1,3},{2,4},{3,5},{4,6},{5,7},{6,0},{7,1},{8,10},{9,11},{10,... | collective-permute-start | bytes 786440 | tf_op jit(solution)/shard_map/ppermute | solution.py:31
  130.0 21.8 %all-to-all-start.2 = ((f32[64,8,512]{2,1,0:T(8,128)}), f32[64,8,512]{2,1,0:T(8,128)S(1)}, u32[]{:S(2)}, u32[]{:S(2)}) async-start(f32[64,8,512]{2,1,0:T(8,128)} %bitcast.31), calls=%async_computation.2 | async-start | bytes 2097152 | tf_op jit(solution)/shard_map/all_to_all | solution.py:253
  153.8 21.0 %all-to-all-start.3 = ((f32[64,8,512]{2,1,0:T(8,128)}), f32[64,8,512]{2,1,0:T(8,128)S(1)}, u32[]{:S(2)}, u32[]{:S(2)}) async-start(f32[64,8,512]{2,1,0:T(8,128)} %broadcast_in_dim.2), calls=%async_computation.3 | async-start | bytes 2097152 | tf_op jit(solution)/shard_map/all_to_all | solution.py:257
  158.6 22.6 %collective-permute-start.30 = (f32[2,128,256]{2,1,0:T(8,128)S(1)}, f32[2,128,256]{2,1,0:T(8,128)S(1)}, u32[]{:S(2)}, u32[]{:S(2)}) collective-permute-start(f32[2,128,256]{2,1,0:T(8,128)S(1)} %get-tuple-element.58), channel_id=1, source_target_pairs={{0,8},{1,9},{2,10},{3,11},{4,12},{5,13},{6,14},{7,15},{8,0},{9,1},... | collective-permute-start | bytes 786440 | tf_op jit(solution)/shard_map/ppermute | solution.py:39
  159.7 21.5 %collective-permute-start.31 = (f32[2,128,256]{2,1,0:T(8,128)S(1)}, f32[2,128,256]{2,1,0:T(8,128)S(1)}, u32[]{:S(2)}, u32[]{:S(2)}) collective-permute-start(f32[2,128,256]{2,1,0:T(8,128)S(1)} %get-tuple-element.60), channel_id=1, source_target_pairs={{0,2},{1,3},{2,4},{3,5},{4,6},{5,7},{6,0},{7,1},{8,10},{9,11},{10,... | collective-permute-start | bytes 786440 | tf_op jit(solution)/shard_map/ppermute | solution.py:31
  160.9 20.3 %collective-permute-start.32 = (f32[2,128,256]{2,1,0:T(8,128)S(1)}, f32[2,128,256]{2,1,0:T(8,128)S(1)}, u32[]{:S(2)}, u32[]{:S(2)}) collective-permute-start(f32[2,128,256]{2,1,0:T(8,128)S(1)} %get-tuple-element.61), channel_id=1, source_target_pairs={{0,6},{1,7},{2,0},{3,1},{4,2},{5,3},{6,4},{7,5},{8,14},{9,15},{10,... | collective-permute-start | bytes 786440 | tf_op jit(solution)/shard_map/ppermute | solution.py:31
  162.4 19.2 %collective-permute-start.33 = (f32[2,128,256]{2,1,0:T(8,128)S(1)}, f32[2,128,256]{2,1,0:T(8,128)}, u32[]{:S(2)}, u32[]{:S(2)}) collective-permute-start(f32[2,128,256]{2,1,0:T(8,128)S(1)} %get-tuple-element.62), channel_id=1, source_target_pairs={{0,4},{1,5},{2,6},{3,7},{4,0},{5,1},{6,2},{7,3},{8,12},{9,13},{10,... | collective-permute-start | bytes 786440 | tf_op jit(solution)/shard_map/ppermute | solution.py:31
  174.8 13.7 %collective-permute-start.35 = (f32[512,512]{1,0:T(8,128)S(1)}, f32[512,512]{1,0:T(8,128)S(1)}, u32[]{:S(2)}, u32[]{:S(2)}) collective-permute-start(f32[512,512]{1,0:T(8,128)S(1)} %bitcast.50), channel_id=1, source_target_pairs={{0,1},{1,0},{2,3},{3,2},{4,5},{5,4},{6,7},{7,6},{8,9},{9,8},{10,11... | collective-permute-start | bytes 3145736 | tf_op jit(solution)/shard_map/ppermute | solution.py:27
  (9 other events, 107.8 us)
